TPU v7x, 256 devices: a whole 4x4x8 slice. The times are simulated.
256 devices in a mesh: narrow: 16 (over z, core), wide: 16 (over x, y).
Axes of the slice: x: 4, y: 4, z: 8, core: 2. Of those that a mesh axis runs over, the one named last changes fastest.
Arguments:
- inputs: bfloat16 [2048, 8192], P('narrow', 'wide'), may hold values from -6 to 6
- gate_blocks: bfloat16 [112, 16, 128, 128], P('wide', 'narrow'), may hold values from -0.125 to 0.125
- up_blocks: bfloat16 [112, 16, 128, 128], P('wide', 'narrow'), may hold values from -0.125 to 0.125
- pattern: int32 [112, 16], P('wide'), may hold values from 0 to 63, as said below
- grad_hidden: bfloat16 [2048, 14336], P('narrow', 'wide'), may hold values from -0.59765625 to 0.59765625
Outputs:
- hidden: bfloat16 [2048, 14336], P('narrow', 'wide')
- grad_inputs: bfloat16 [2048, 8192], P('narrow', 'wide')
- grad_gate: bfloat16 [112, 16, 128, 128], P('wide', 'narrow')
- grad_up: bfloat16 [112, 16, 128, 128], P('wide', 'narrow')
Inputs may be any that keep to these rules, and one draw needn't show every extreme that they name: pattern[j, k] = b_j XOR m_k, with one offset b_j for each block column and 16 distinct masks m_k common to all block columns, so each block column lists 16 distinct block rows.
All inputs are finite; a program needn't handle non-finite values.
Results may differ from a plain program's by a relative error of at most 0.023.
Values may be sent and summed in bfloat16 or wider, within the bound.
A program may use at most 128 MiB of HBM per device.

v0:
```python
import jax
import jax.numpy as jnp
from jax import lax
from jax.sharding import PartitionSpec as P


def silu_parts(gate_sum):
    sigmoid_value = jax.nn.sigmoid(gate_sum)
    return (gate_sum * sigmoid_value, sigmoid_value * (1.0 + gate_sum * (1.0 - sigmoid_value)))


def shards(inputs, gate_blocks, up_blocks, pattern, grad_hidden):
    tokens_here = inputs.shape[0]
    block_size = gate_blocks.shape[2]
    columns = gate_blocks.shape[0]
    full_inputs = lax.all_gather(inputs, "wide", axis=1, tiled=True)
    row_blocks = full_inputs.shape[1] // block_size
    input_blocks = full_inputs.reshape(tokens_here, row_blocks, block_size)

    def picks_for():
        return jnp.take(input_blocks, pattern, axis=1)

    gate_all, up_all = (
        lax.all_gather(gate_blocks, "narrow", axis=1, tiled=True),
        lax.all_gather(up_blocks, "narrow", axis=1, tiled=True),
    )
    pieces = (gate_all, up_all)
    picked = picks_for()
    gate_sum = jnp.einsum("tjkb,jkbc->tjc", picked, pieces[0], preferred_element_type=jnp.float32)
    up_sum = jnp.einsum("tjkb,jkbc->tjc", picked, pieces[1], preferred_element_type=jnp.float32)
    gate_sum, up_sum = (gate_sum, up_sum)
    activation, derivative = silu_parts(gate_sum)
    hidden = (activation * up_sum).astype(jnp.bfloat16)
    cotangent = grad_hidden.reshape(tokens_here, columns, block_size).astype(jnp.float32)
    d_gate = (cotangent * up_sum * derivative).astype(jnp.bfloat16)
    d_up = (cotangent * activation).astype(jnp.bfloat16)
    zero_inputs = jnp.zeros((tokens_here, row_blocks, block_size), jnp.float32)
    pieces = (gate_all, up_all)
    number_slots = pieces[0].shape[1]

    def one_slot(k, running):
        gate_slot = lax.dynamic_index_in_dim(pieces[0], k, 1, keepdims=False)
        up_slot = lax.dynamic_index_in_dim(pieces[1], k, 1, keepdims=False)
        contribution = jnp.einsum(
            "tjc,jbc->tjb", d_gate, gate_slot, preferred_element_type=jnp.float32
        )
        contribution = contribution + jnp.einsum(
            "tjc,jbc->tjb", d_up, up_slot, preferred_element_type=jnp.float32
        )
        targets = lax.dynamic_index_in_dim(pattern, k, 1, keepdims=False)
        return running.at[:, targets].add(contribution)

    partial_inputs = lax.fori_loop(0, number_slots, one_slot, zero_inputs)
    grad_inputs = lax.psum_scatter(
        partial_inputs.reshape(tokens_here, row_blocks * block_size).astype(jnp.bfloat16),
        "wide",
        scatter_dimension=1,
        tiled=True,
    )
    picked_all = picks_for()
    gate_terms = jnp.einsum(
        "tjkb,tjc->jkbc", picked_all, d_gate, preferred_element_type=jnp.float32
    )
    up_terms = jnp.einsum("tjkb,tjc->jkbc", picked_all, d_up, preferred_element_type=jnp.float32)
    grad_gate, grad_up = (
        lax.psum_scatter(
            gate_terms.astype(jnp.bfloat16), "narrow", scatter_dimension=1, tiled=True
        ).astype(jnp.float32),
        lax.psum_scatter(
            up_terms.astype(jnp.bfloat16), "narrow", scatter_dimension=1, tiled=True
        ).astype(jnp.float32),
    )
    return (
        hidden.reshape(tokens_here, columns * block_size),
        grad_inputs,
        grad_gate.astype(jnp.bfloat16),
        grad_up.astype(jnp.bfloat16),
    )


def solution(mesh):
    placed = (
        P("narrow", "wide"),
        P("wide", "narrow", None, None),
        P("wide", "narrow", None, None),
        P("wide", None),
        P("narrow", "wide"),
    )
    return jax.shard_map(
        shards,
        mesh=mesh,
        in_specs=placed,
        out_specs=(
            P("narrow", "wide"),
            P("narrow", "wide"),
            P("wide", "narrow", None, None),
            P("wide", "narrow", None, None),
        ),
        check_vma=False,
    )
```

profile of v0, /device:TPU:32, one launch (start us, length us, event | category | flops | bytes accessed | tf_op | source)
XLA Modules:
  0.0 384.9 jit_solution(9591232748475014344)
XLA Ops:
  7.2 1.7 copy.60
  8.9 1.8 copy.65
  10.8 1.8 copy.63
  16.0 47.6 %all-gather.4.cloned.1.call-done = bf16[128,8192]{0,1:T(8,128)(2,1)} async-done(((bf16[128,512]{0,1:T(8,128)(2,1)}), bf16[128,8192]{0,1:T(8,128)(2,1)}) %all-gather.4.cloned.1.call-update) | async-done | bytes 2097168 | tf_op jit(solution)/shard_map/all_gather | solution.py:16
  63.6 3.2 copy.61
  66.8 3.0 gather_fusion
  69.8 6.1 %copy.62 = bf16[7,16,128,128]{2,3,1,0:T(8,128)(2,1)} copy(bf16[7,16,128,128]{3,2,1,0:T(8,128)(2,1)} %bitcast.89) | data formatting | bytes 7340032 | tf_op jit(solution)/shard_map/jit(_take)/gather | solution.py:21
  75.9 31.0 %all-gather.8.cloned.1.call-done = bf16[7,16,128,128]{2,3,1,0:T(8,128)(2,1)} async-done(((bf16[7,1,128,128]{2,3,1,0:T(8,128)(2,1)}), bf16[7,16,128,128]{2,3,1,0:T(8,128)(2,1)}) %all-gather.8.cloned.1.call-update) | async-done | bytes 3670032 | tf_op jit(solution)/shard_map/all_gather | solution.py:25
  106.9 4.4 %fusion.27 = f32[128,7,128]{0,2,1:T(8,128)S(1)} fusion(bf16[7,16,128,128]{2,3,1,0:T(8,128)(2,1)} %all-gather.8.cloned.1.call-done, bf16[7,16,128,128]{2,3,1,0:T(8,128)(2,1)} %copy.62, pred[7,16]{1,0:T(8,128)(4,1)S(1)} %compare_and_fusion), kind=kOutput, calls=%fused_computation.31 | convolution fusion | flops 471597056 | bytes 7798896 | tf_op jit(solution)/shard_map/tjkb,jkbc->tjc/dot_general | solution.py:30
  111.3 38.3 %all-gather.6.cloned.1.call-done = bf16[7,16,128,128]{2,3,1,0:T(8,128)(2,1)} async-done(((bf16[7,1,128,128]{2,3,1,0:T(8,128)(2,1)}), bf16[7,16,128,128]{2,3,1,0:T(8,128)(2,1)}) %all-gather.6.cloned.1.call-update) | async-done | bytes 3670032 | tf_op jit(solution)/shard_map/all_gather | solution.py:24
  149.6 4.5 %multiply_convert_fusion = (bf16[128,7,128]{0,2,1:T(8,128)(2,1)S(1)}, bf16[128,7,128]{0,2,1:T(8,128)(2,1)S(1)}, bf16[128,7,128]{0,2,1:T(8,128)(2,1)S(1)}) fusion(f32[128,7,128]{0,2,1:T(8,128)S(1)} %bitcast.91, f32[128,7,128]{0,2,1:T(8,128)S(1)} %fusion.27, bf16[7,16,128,128]{2,3,1,0:T(8,128)(2,1)} %all-gather.6.cloned.1.call-done, ...), kind=kOutput, calls=%fused_computation.33 | convolution fusion | flops 473317376 | bytes 8945776 | tf_op jit(solution)/shard_map/tjkb,jkbc->tjc/dot_general | solution.py:29
  154.3 5.1 %fusion.17 = bf16[7,16,128,128]{3,2,1,0:T(8,128)(2,1)} fusion(bf16[7,16,128,128]{2,3,1,0:T(8,128)(2,1)} %copy.62, pred[7,16]{1,0:T(8,128)(4,1)S(1)} %compare_and_fusion, bf16[128,7,128]{0,2,1:T(8,128)(2,1)S(1)} %get-tuple-element.191), kind=kOutput, calls=%fused_computation.23 | convolution fusion | flops 473432064 | bytes 7569520 | tf_op jit(solution)/shard_map/tjkb,tjc->jkbc/dot_general | solution.py:61
  159.6 5.0 %fusion.20 = bf16[7,16,128,128]{3,2,1,0:T(8,128)(2,1)} fusion(bf16[7,16,128,128]{2,3,1,0:T(8,128)(2,1)} %copy.62, pred[7,16]{1,0:T(8,128)(4,1)S(1)} %compare_and_fusion, bf16[128,7,128]{0,2,1:T(8,128)(2,1)S(1)} %get-tuple-element.190), kind=kOutput, calls=%fused_computation.24 | convolution fusion | flops 473432064 | bytes 7569520 | tf_op jit(solution)/shard_map/tjkb,tjc->jkbc/dot_general | solution.py:64
  164.7 2.5 broadcast_in_dim.15
  167.1 86.0 %while.13 = (s32[]{:T(128)}, f32[128,64,128]{2,0,1:T(8,128)}, s32[7,16]{0,1:T(8,128)S(1)}, bf16[7,16,128,128]{2,3,1,0:T(8,128)(2,1)}, bf16[128,7,128]{2,0,1:T(8,...) while((s32[]{:T(128)}, f32[128,64,128]{2,0,1:T(8,128)}, ...), condition=%wide.region_2.4_spmd, body=%wide.region_0.3_spmd.sunk | while | flops 58949656 | bytes 4587709 | solution.py:53
  167.2 1.2 fusion.56
  168.4 1.3 fusion.57
  169.9 2.6 scatter_fusion
  173.7 1.3 fusion.57
  175.2 2.7 scatter_fusion
  177.9 1.2 fusion.56
  179.2 1.3 fusion.57
  180.6 2.7 scatter_fusion
  183.3 1.2 fusion.56
  184.5 1.3 fusion.57
  186.0 2.7 scatter_fusion
  188.7 1.3 fusion.56
  189.9 1.3 fusion.57
  191.4 2.7 scatter_fusion
  195.3 1.3 fusion.57
  196.8 2.7 scatter_fusion
  199.4 1.3 fusion.56
  200.7 1.3 fusion.57
  202.1 2.7 scatter_fusion
  204.8 1.2 fusion.56
  206.1 1.3 fusion.57
  207.5 2.7 scatter_fusion
  210.2 1.2 fusion.56
  211.4 1.3 fusion.57
  212.9 2.6 scatter_fusion
  215.6 1.2 fusion.56
  216.8 1.3 fusion.57
  218.3 2.6 scatter_fusion
  220.9 1.3 fusion.56
  222.2 1.3 fusion.57
  223.6 2.6 scatter_fusion
  226.3 1.3 fusion.56
  227.5 1.3 fusion.57
  229.0 2.6 scatter_fusion
  232.9 1.3 fusion.57
  234.3 2.6 scatter_fusion
  237.0 1.2 fusion.56
  238.2 1.3 fusion.57
  239.7 2.7 scatter_fusion
  242.4 1.3 fusion.56
  243.6 1.3 fusion.57
  245.1 2.7 scatter_fusion
  247.8 1.2 fusion.56
  249.0 1.3 fusion.57
  250.5 2.7 scatter_fusion
  253.1 3.9 %copy_bitcast_fusion = bf16[128,8192]{1,0:T(8,128)(2,1)} fusion(f32[128,64,128]{2,0,1:T(8,128)} %get-tuple-element.129), kind=kLoop, calls=%fused_computation.25 | loop fusion | flops 1048576 | bytes 6291456 | tf_op jit(solution)/shard_map/convert_element_type | solution.py:55
  258.5 34.1 %all-reduce.5.cloned.1.call-done = (bf16[7,16,128,128]{3,2,1,0:T(8,128)(2,1)}, bf16[7,16,128,128]{3,2,1,0:T(8,128)(2,1)}) async-done(((bf16[7,16,128,128]{3,2,1,0:T(8,128)(2,1)}, bf16[7,16,128,128]{3,2,1,0:T(8,128)(2,1)}), (bf16[7,16,128,128]{3,2,1,0:T(8,128)(2,1)}, bf16[7,16,128,128]{3,2,1,0:T(8,128)(2,1)})) %all-reduce.5.cloned.1.call-update) | async-done | bytes 7340048
  292.6 2.5 constant_dynamic-slice_fusion.1
  295.1 83.3 %reduce-scatter.8.cloned.1.call-done = bf16[128,512]{1,0:T(8,128)(2,1)} async-done(((bf16[128,8192]{1,0:T(8,128)(2,1)}), bf16[128,512]{1,0:T(8,128)(2,1)}) %reduce-scatter.8.cloned.1.call-update) | async-done | bytes 131088 | tf_op jit(solution)/shard_map/reduce_scatter | solution.py:54
  (57 shorter events, 12.4 us)
Async XLA Ops:
  7.2 56.4 %all-gather.4.cloned.1.call-start = ((), (), s32[]{:S(2)}) async-start(), calls=%async_computation.1 | async-start | bytes 2228224 | tf_op jit(solution)/shard_map/all_gather | solution.py:16
  8.9 98.0 %all-gather.8.cloned.1.call-start = ((), (), s32[]{:S(2)}) async-start(), calls=%async_computation.3 | async-start | bytes 3899392 | tf_op jit(solution)/shard_map/all_gather | solution.py:25
  10.7 138.8 %all-gather.6.cloned.1.call-start = ((), (), s32[]{:S(2)}) async-start(), calls=%async_computation.2 | async-start | bytes 3899392 | tf_op jit(solution)/shard_map/all_gather | solution.py:24
  12.6 280.0 %all-reduce.5.cloned.1.call-start = ((), (), s32[]{:S(2)}) async-start(), calls=%async_computation.5 | async-start | bytes 14680064
  164.6 213.7 %reduce-scatter.8.cloned.1.call-start = ((), (), s32[]{:S(2)}) async-start(), calls=%async_computation.4 | async-start | bytes 2228224 | tf_op jit(solution)/shard_map/reduce_scatter | solution.py:54
  253.1 3.9 %copy-start = (u32[256]{0:T(256)S(1)}, u32[256]{0:T(256)}, u32[]{:S(2)}) copy-start(u32[256]{0:T(256)} %constant.58) | copy-start | bytes 3076
Sparse Core Ops, SparseCore 0:
  11.0 52.5 all-gather.3
  66.0 40.8 all-gather.7
  109.3 40.2 all-gather.5
  164.7 127.8 all-reduce.4
  296.6 81.7 reduce-scatter.7
where the time goes:
time: 387 us; the launch traced here: 385 us
  waiting for transfers between devices  234 us (60%)
  matrix products  59.2 us (15%)
  other arithmetic  47.8 us (12%)
  local copies, waits for them, and re-layouts  29.3 us (8%)
  between operations  13.8 us (4%)
    reduce_scatter x1, waiting for transfers between devices, shards(): lax.psum_scatter(partial_inputs.reshape(tokens_here, row_blocks * block_s...  83.3 us
    all_gather x1, waiting for transfers between devices, shards(): full_inputs = lax.all_gather(inputs, 'wide', axis=1, tiled=True)  47.6 us
    scatter-add x16, other arithmetic, one_slot(): return running.at[:, targets].add(contribution)  42.4 us
    all_gather x1, waiting for transfers between devices, shards(): lax.all_gather(gate_blocks, 'narrow', axis=1, tiled=True)  38.3 us
    unnamed x6, waiting for transfers between devices  34.2 us
    all_gather x1, waiting for transfers between devices, shards(): lax.all_gather(up_blocks, 'narrow', axis=1, tiled=True)  31 us
    dot_general x16, matrix products, one_slot(): jnp.einsum('tjc,jbc->tjb', d_up, up_slot, preferred_element_type=jnp.floa...  20.2 us
    dot_general x16, matrix products, one_slot(): jnp.einsum('tjc,jbc->tjb', d_gate, gate_slot, preferred_element_type=jnp....  20 us
  transfers between devices with their start and end apart: 5, of which 5 were waited for; matrix products, arithmetic and copies ran while one was open for 31% of the time, Pallas kernels for 0%

commit v1 on v0

--- a/solution.py
+++ b/solution.py
@@ -13,7 +13,10 @@
     tokens_here = inputs.shape[0]
     block_size = gate_blocks.shape[2]
     columns = gate_blocks.shape[0]
-    full_inputs = lax.all_gather(inputs, "wide", axis=1, tiled=True)
+    size = lax.axis_size("wide")
+    blocks = jnp.stack([inputs for _ in range(size)])
+    blocks = lax.all_to_all(blocks, "wide", split_axis=0, concat_axis=0)
+    full_inputs = jnp.concatenate(blocks, axis=1)
     row_blocks = full_inputs.shape[1] // block_size
     input_blocks = full_inputs.reshape(tokens_here, row_blocks, block_size)
 

time: 387 us -> 335 us (0.87)
  waiting for transfers between devices: 234 us -> 175 us
  starting transfers between devices: 0.21 us -> 7.2 us
    all_gather x1 -> x0, waiting for transfers between devices: 47.6 us -> none  [shards(): full_inputs = lax.all_gather(inputs, 'wide', axis=1, tiled=True)]
    all_gather x1, waiting for transfers between devices: 31 us -> 0.01 us  [shards(): lax.all_gather(up_blocks, 'narrow', axis=1, tiled=True)]
    all_to_all x0 -> x1, waiting for transfers between devices: none -> 30 us  [shards(): blocks = lax.all_to_all(blocks, 'wide', split_axis=0, concat_axis=0)]
    all_gather x1, waiting for transfers between devices: 38.3 us -> 27.9 us  [shards(): lax.all_gather(gate_blocks, 'narrow', axis=1, tiled=True)]
    all_to_all x0 -> x1, starting transfers between devices: none -> 7.03 us  [shards(): blocks = lax.all_to_all(blocks, 'wide', split_axis=0, concat_axis=0)]
    another operation x0 -> x2, local copies, waits for them, and re-layouts: none -> 4.97 us  [the longest x1 3.22 us: shards(): input_blocks = full_inputs.reshape(tokens_here, row_blocks, block_size)]
    unnamed x8 -> x14, local copies, waits for them, and re-layouts: 9.13 us -> 9.9 us
    unnamed x6 -> x5, waiting for transfers between devices: 34.2 us -> 34.1 us
  transfers between devices with their start and end apart: 5 -> 5, of which waited for: 5 -> 4; matrix products, arithmetic and copies ran while one was open for 31% -> 35% of each run, Pallas kernels for 0% -> 0%
where the time goes in v1:
time: 335 us; the launch traced here: 333 us
  waiting for transfers between devices  175 us (52%)
  matrix products  59.4 us (18%)
  other arithmetic  46.5 us (14%)
  local copies, waits for them, and re-layouts  30.2 us (9%)
  between operations  13.9 us (4%)
  starting transfers between devices  7.2 us (2%)
    reduce_scatter x1, waiting for transfers between devices, shards(): lax.psum_scatter(partial_inputs.reshape(tokens_here, row_blocks * block_s...  83.3 us
    scatter-add x16, other arithmetic, one_slot(): return running.at[:, targets].add(contribution)  42.5 us
    unnamed x5, waiting for transfers between devices  34.1 us
    all_to_all x1, waiting for transfers between devices, shards(): blocks = lax.all_to_all(blocks, 'wide', split_axis=0, concat_axis=0)  30 us
    all_gather x1, waiting for transfers between devices, shards(): lax.all_gather(gate_blocks, 'narrow', axis=1, tiled=True)  27.9 us
    dot_general x16, matrix products, one_slot(): jnp.einsum('tjc,jbc->tjb', d_up, up_slot, preferred_element_type=jnp.floa...  20.2 us
    dot_general x16, matrix products, one_slot(): jnp.einsum('tjc,jbc->tjb', d_gate, gate_slot, preferred_element_type=jnp....  20 us
    unnamed x14, local copies, waits for them, and re-layouts  9.9 us
  transfers between devices with their start and end apart: 5, of which 4 were waited for; matrix products, arithmetic and copies ran while one was open for 35% of the time, Pallas kernels for 0%

profile of v1, /device:TPU:32, one launch (start us, length us, event | category | flops | bytes accessed | tf_op | source)
XLA Modules:
  0.0 332.5 jit_solution(6360533235871033290)
XLA Ops:
  7.2 1.8 copy.48
  9.1 1.8 copy.46
  11.9 1.8 stack.2
  13.7 7.0 %all-to-all-start = ((bf16[16,128,512]{1,2,0:T(8,128)(2,1)}), bf16[16,128,512]{1,2,0:T(8,128)(2,1)S(1)}, u32[]{:S(2)}, u32[]{:S(2)}) async-start(bf16[16,128,512]{1,2,0:T(8,128)(2,1)} %stack.2), calls=%async_computation | async-start | bytes 4194304 | tf_op jit(solution)/shard_map/all_to_all | solution.py:18
  21.1 30.0 %all-to-all-done = bf16[16,128,512]{1,2,0:T(8,128)(2,1)S(1)} async-done(((bf16[16,128,512]{1,2,0:T(8,128)(2,1)}), bf16[16,128,512]{1,2,0:T(8,128)(2,1)S(1)}, u32[]{:S(2)}, u32[]{:S(2)}) %all-to-all-start) | async-done | bytes 2097184 | tf_op jit(solution)/shard_map/all_to_all | solution.py:18
  51.1 1.3 copy-done
  52.5 3.2 copy.44
  55.7 2.9 gather_fusion
  58.6 6.1 %copy.45 = bf16[7,16,128,128]{2,3,1,0:T(8,128)(2,1)} copy(bf16[7,16,128,128]{3,2,1,0:T(8,128)(2,1)} %bitcast.91) | data formatting | bytes 7340032 | tf_op jit(solution)/shard_map/jit(_take)/gather | solution.py:24
  64.8 4.5 %fusion.27 = f32[128,7,128]{0,2,1:T(8,128)S(1)} fusion(bf16[7,16,128,128]{2,3,1,0:T(8,128)(2,1)} %all-gather.5.cloned.1.call-done, bf16[7,16,128,128]{2,3,1,0:T(8,128)(2,1)} %copy.45, pred[7,16]{1,0:T(8,128)(4,1)S(1)} %compare_and_fusion), kind=kOutput, calls=%fused_computation.31 | convolution fusion | flops 471597056 | bytes 7798896 | tf_op jit(solution)/shard_map/tjkb,jkbc->tjc/dot_general | solution.py:33
  69.3 27.9 %all-gather.3.cloned.1.call-done = bf16[7,16,128,128]{2,3,1,0:T(8,128)(2,1)} async-done(((bf16[7,1,128,128]{2,3,1,0:T(8,128)(2,1)}), bf16[7,16,128,128]{2,3,1,0:T(8,128)(2,1)}) %all-gather.3.cloned.1.call-update) | async-done | bytes 3670032 | tf_op jit(solution)/shard_map/all_gather | solution.py:27
  97.2 4.6 %multiply_convert_fusion = (bf16[128,7,128]{0,2,1:T(8,128)(2,1)S(1)}, bf16[128,7,128]{0,2,1:T(8,128)(2,1)S(1)}, bf16[128,7,128]{0,2,1:T(8,128)(2,1)S(1)}) fusion(f32[128,7,128]{0,2,1:T(8,128)S(1)} %bitcast.93, f32[128,7,128]{0,2,1:T(8,128)S(1)} %fusion.27, bf16[7,16,128,128]{2,3,1,0:T(8,128)(2,1)} %all-gather.3.cloned.1.call-done, ...), kind=kOutput, calls=%fused_computation.33 | convolution fusion | flops 473317376 | bytes 8945776 | tf_op jit(solution)/shard_map/tjkb,jkbc->tjc/dot_general | solution.py:32
  101.9 5.1 %fusion.17 = bf16[7,16,128,128]{3,2,1,0:T(8,128)(2,1)} fusion(bf16[7,16,128,128]{2,3,1,0:T(8,128)(2,1)} %copy.45, pred[7,16]{1,0:T(8,128)(4,1)S(1)} %compare_and_fusion, bf16[128,7,128]{0,2,1:T(8,128)(2,1)S(1)} %get-tuple-element.180), kind=kOutput, calls=%fused_computation.23 | convolution fusion | flops 473432064 | bytes 7569520 | tf_op jit(solution)/shard_map/tjkb,tjc->jkbc/dot_general | solution.py:64
  107.2 5.0 %fusion.20 = bf16[7,16,128,128]{3,2,1,0:T(8,128)(2,1)} fusion(bf16[7,16,128,128]{2,3,1,0:T(8,128)(2,1)} %copy.45, pred[7,16]{1,0:T(8,128)(4,1)S(1)} %compare_and_fusion, bf16[128,7,128]{0,2,1:T(8,128)(2,1)S(1)} %get-tuple-element.179), kind=kOutput, calls=%fused_computation.24 | convolution fusion | flops 473432064 | bytes 7569520 | tf_op jit(solution)/shard_map/tjkb,tjc->jkbc/dot_general | solution.py:67
  112.3 2.5 broadcast_in_dim.15
  114.7 86.1 %while.13 = (s32[]{:T(128)}, f32[128,64,128]{2,0,1:T(8,128)}, s32[7,16]{0,1:T(8,128)S(1)}, bf16[7,16,128,128]{2,3,1,0:T(8,128)(2,1)}, bf16[128,7,128]{2,0,1:T(8,...) while((s32[]{:T(128)}, f32[128,64,128]{2,0,1:T(8,128)}, ...), condition=%wide.region_2.4_spmd, body=%wide.region_0.3_spmd.sunk | while | flops 58949656 | bytes 4587709 | solution.py:56
  116.0 1.3 fusion.57
  117.4 2.6 scatter_fusion
  120.1 1.2 fusion.56
  121.3 1.3 fusion.57
  122.8 2.7 scatter_fusion
  125.5 1.3 fusion.56
  126.8 1.3 fusion.57
  128.2 2.7 scatter_fusion
  130.9 1.2 fusion.56
  132.1 1.3 fusion.57
  133.6 2.7 scatter_fusion
  136.3 1.3 fusion.56
  137.5 1.3 fusion.57
  139.0 2.7 scatter_fusion
  141.7 1.3 fusion.56
  142.9 1.3 fusion.57
  144.4 2.7 scatter_fusion
  147.0 1.3 fusion.56
  148.3 1.3 fusion.57
  149.8 2.6 scatter_fusion
  152.4 1.3 fusion.56
  153.7 1.3 fusion.57
  155.1 2.7 scatter_fusion
  159.1 1.3 fusion.57
  160.5 2.7 scatter_fusion
  163.2 1.3 fusion.56
  164.4 1.3 fusion.57
  165.9 2.6 scatter_fusion
  168.5 1.3 fusion.56
  169.8 1.3 fusion.57
  171.3 2.6 scatter_fusion
  173.9 1.3 fusion.56
  175.2 1.3 fusion.57
  176.6 2.6 scatter_fusion
  180.5 1.3 fusion.57
  182.0 2.6 scatter_fusion
  185.9 1.3 fusion.57
  187.3 2.7 scatter_fusion
  190.0 1.3 fusion.56
  191.3 1.3 fusion.57
  192.7 2.7 scatter_fusion
  195.4 1.3 fusion.56
  196.7 1.3 fusion.57
  198.2 2.6 scatter_fusion
  200.8 3.9 %copy_bitcast_fusion = bf16[128,8192]{1,0:T(8,128)(2,1)} fusion(f32[128,64,128]{2,0,1:T(8,128)} %get-tuple-element.129), kind=kLoop, calls=%fused_computation.25 | loop fusion | flops 1048576 | bytes 6291456 | tf_op jit(solution)/shard_map/convert_element_type | solution.py:58
  206.2 34.0 %all-reduce.5.cloned.1.call-done = (bf16[7,16,128,128]{3,2,1,0:T(8,128)(2,1)}, bf16[7,16,128,128]{3,2,1,0:T(8,128)(2,1)}) async-done(((bf16[7,16,128,128]{3,2,1,0:T(8,128)(2,1)}, bf16[7,16,128,128]{3,2,1,0:T(8,128)(2,1)}), (bf16[7,16,128,128]{3,2,1,0:T(8,128)(2,1)}, bf16[7,16,128,128]{3,2,1,0:T(8,128)(2,1)})) %all-reduce.5.cloned.1.call-update) | async-done | bytes 7340048
  240.2 2.5 constant_dynamic-slice_fusion.1
  242.7 83.3 %reduce-scatter.8.cloned.1.call-done = bf16[128,512]{1,0:T(8,128)(2,1)} async-done(((bf16[128,8192]{1,0:T(8,128)(2,1)}), bf16[128,512]{1,0:T(8,128)(2,1)}) %reduce-scatter.8.cloned.1.call-update) | async-done | bytes 131088 | tf_op jit(solution)/shard_map/reduce_scatter | solution.py:57
  (63 shorter events, 11.7 us)
Async XLA Ops:
  7.2 57.6 %all-gather.5.cloned.1.call-start = ((), (), s32[]{:S(2)}) async-start(), calls=%async_computation.3 | async-start | bytes 3899392 | tf_op jit(solution)/shard_map/all_gather | solution.py:28
  9.0 11.8 %copy-start.1 = (bf16[128,896]{1,0:T(8,128)(2,1)S(1)}, bf16[128,896]{1,0:T(8,128)(2,1)}, u32[]{:S(2)}) copy-start(bf16[128,896]{1,0:T(8,128)(2,1)} %param.13) | copy-start | bytes 688132
  9.0 88.2 %all-gather.3.cloned.1.call-start = ((), (), s32[]{:S(2)}) async-start(), calls=%async_computation.2 | async-start | bytes 3899392 | tf_op jit(solution)/shard_map/all_gather | solution.py:27
  10.9 10.0 %copy-start.2 = (s32[7,16]{1,0:T(8,128)S(1)}, s32[7,16]{1,0:T(8,128)}, u32[]{:S(2)}) copy-start(s32[7,16]{1,0:T(8,128)} %param.12) | copy-start | bytes 1348
  13.7 37.4 %all-to-all-start = ((bf16[16,128,512]{1,2,0:T(8,128)(2,1)}), bf16[16,128,512]{1,2,0:T(8,128)(2,1)S(1)}, u32[]{:S(2)}, u32[]{:S(2)}) async-start(bf16[16,128,512]{1,2,0:T(8,128)(2,1)} %stack.2), calls=%async_computation | async-start | bytes 4194304 | tf_op jit(solution)/shard_map/all_to_all | solution.py:18
  20.7 219.5 %all-reduce.5.cloned.1.call-start = ((), (), s32[]{:S(2)}) async-start(), calls=%async_computation.5 | async-start | bytes 14680064
  51.1 1.3 copy-start
  112.2 213.8 %reduce-scatter.8.cloned.1.call-start = ((), (), s32[]{:S(2)}) async-start(), calls=%async_computation.4 | async-start | bytes 2228224 | tf_op jit(solution)/shard_map/reduce_scatter | solution.py:57
  200.8 3.9 %copy-start.3 = (u32[256]{0:T(256)S(1)}, u32[256]{0:T(256)}, u32[]{:S(2)}) copy-start(u32[256]{0:T(256)} %constant.58) | copy-start | bytes 3076
Sparse Core Ops, SparseCore 0:
  10.4 44.0 all-gather.4
  56.9 40.2 all-gather.2
  112.3 127.8 all-reduce.4
  244.2 81.7 reduce-scatter.7
